TPU v7x, 256 devices: a whole 4x4x8 slice. The times are simulated.
256 devices in a mesh: ctx: 64 (over x_hi, y, z), tp: 4 (over x_lo, core).
Axes of the slice: x: 4 (x_hi: 2, x_lo: 2; x = x_hi * 2 + x_lo), y: 4, z: 8, core: 2. Of those that a mesh axis runs over, the one named last changes fastest.
Arguments:
- hidden: bfloat16 [16384, 2048], P('ctx', 'tp'), may hold values from -6 to 6
- norm_gain_a: float32 [2048], replicated, may hold values from 0.5 to 1.5
- in_weight_a: bfloat16 [3, 2048, 2048], P(None, 'ctx', 'tp'), may hold values from -0.125 to 0.125
- mr_filter: bfloat16 [128, 128], P('tp'), may hold values from -0.5 to 0.5
- out_weight_a: bfloat16 [2048, 2048], P('tp', 'ctx'), may hold values from -0.125 to 0.125
- norm_gain_b: float32 [2048], replicated, may hold values from 0.5 to 1.5
- in_weight_b: bfloat16 [3, 2048, 2048], P(None, 'ctx', 'tp'), may hold values from -0.125 to 0.125
- li_rate: float32 [128, 16], P('tp'), may hold values from 6.1035156e-06 to 0.0333333333
- li_residue: float32 [128, 16], P('tp'), may hold values from -3 to 3
- out_weight_b: bfloat16 [2048, 2048], P('tp', 'ctx'), may hold values from -0.125 to 0.125
Outputs:
- mixed: bfloat16 [16384, 2048], P('ctx', 'tp')
- gated_medium: bfloat16 [2048, 16384], P('tp', 'ctx')
- gated_long: bfloat16 [2048, 16384], P('tp', 'ctx')
All inputs are finite; a program needn't handle non-finite values.
Results may differ from a plain program's by a relative error of at most 0.02.
Values may be sent and summed in bfloat16 or wider, within the bound.
No kernel may reach another device: no remote copies, remote signals or barrier semaphores. Data moves between devices by JAX's collectives and lax.ppermute only.
A program may use at most 64 MiB of HBM per device.

v0:
```python
import jax
import jax.numpy as jnp
from jax import lax
from jax.sharding import Mesh
from jax.sharding import PartitionSpec as P

GROUP = 16
TAPS = 128
CTX = ("ctx_0", "ctx_1", "ctx_2")


def laid_out(blocks, dim):
    blocks = jnp.moveaxis(blocks, 0, dim)
    dims = blocks.shape
    return blocks.reshape(*dims[:dim], dims[dim] * dims[dim + 1], *dims[dim + 2 :])


def gather_in_order(shard, axes, order):
    blocks = shard[None]
    for k in order:
        blocks = lax.all_gather(blocks, axes[k], axis=0, tiled=True)
    current = [lax.axis_size(axes[k]) for k in reversed(order)]
    blocks = blocks.reshape(*current, *shard.shape)
    turned = sorted(range(len(order)), key=lambda place: order[len(order) - 1 - place])
    return blocks.transpose(*turned, *range(len(order), blocks.ndim)).reshape(-1, *shard.shape)


def gathered_by_axis(shard, axes, order, dim):
    return laid_out(gather_in_order(shard, axes, order), dim)


def passed_along(value, axis, steps):
    count = lax.axis_size(axis)
    initial, last = (max(0, -steps), min(count, count - steps))
    return lax.ppermute(value, axis, [(source, source + steps) for source in range(initial, last)])


def from_everyone(shard, axis):
    copies = jnp.broadcast_to(shard, (lax.axis_size(axis), *shard.shape))
    return lax.all_to_all(copies, axis, split_axis=0, concat_axis=0, tiled=True)


def collect(shard, axis, dim):
    return laid_out(from_everyone(shard, axis), dim)


def cut_along(shard, dim, peers):
    before, after = (shard.shape[:dim], shard.shape[dim + 1 :])
    return jnp.moveaxis(shard.reshape(*before, peers, -1, *after), dim, 0)


def sent_and_summed(shard, axis, dim):
    peers = lax.axis_size(axis)
    blocks = lax.all_to_all(cut_along(shard, dim, peers), axis, 0, 0, tiled=True)
    return jnp.sum(blocks.astype(jnp.float32), axis=0)


def normalize(values, gain):
    widened = values.astype(jnp.float32)
    factor = lax.rsqrt(jnp.mean(widened * widened, axis=1, keepdims=True) + 1e-06)
    return (widened * factor * gain).astype(jnp.bfloat16)


def layer_inputs(gathered, gain, weight):
    normed = normalize(gathered, gain)
    projected = jnp.einsum(
        "knc,tn->kct",
        gathered_by_axis(weight, CTX, (0, 1, 2), 1),
        normed,
        preferred_element_type=jnp.float32,
    )
    return (projected[1], (projected[0] * projected[2]).astype(jnp.bfloat16))


def out_project(gated, weight):
    return jnp.einsum(
        "ct,cn->tn",
        gated,
        lax.all_gather(weight, CTX, axis=1, tiled=True),
        preferred_element_type=jnp.float32,
    )


def toeplitz_rows(filters):
    group_count, tap_count = filters.shape
    padded_filter = jnp.concatenate(
        [
            jnp.zeros((group_count, 1), filters.dtype),
            filters[:, ::-1],
            jnp.zeros((group_count, tap_count), filters.dtype),
        ],
        axis=1,
    )
    tiled = jnp.tile(padded_filter, (1, tap_count))[:, : tap_count * 2 * tap_count]
    return tiled.reshape(group_count, tap_count, 2 * tap_count)


def medium_conv(medium_in, mr_filter):
    channels_here, tokens_here = medium_in.shape
    prior_rim = passed_along(medium_in[:, tokens_here - TAPS :], CTX, 1)
    extended = jnp.concatenate([prior_rim, medium_in], axis=1)
    group_count = channels_here // GROUP
    block_count = tokens_here // TAPS
    grouped = extended.reshape(group_count, GROUP, block_count + 1, TAPS)
    windows = jnp.concatenate([grouped[:, :, :-1], grouped[:, :, 1:]], axis=3)
    filter_rows = toeplitz_rows(mr_filter)
    result = jnp.einsum("gts,gkbs->gkbt", filter_rows, windows, preferred_element_type=jnp.float32)
    return result.reshape(channels_here, tokens_here)


def chain_blocks(earlier, latter):
    return (earlier[0] * latter[1] + latter[0], earlier[1] * latter[1])


def long_parts(values, decay_rates, residues):
    group_count, per_group, length = values.shape
    block_count = length // TAPS
    blocks = values.astype(jnp.float32).reshape(group_count, per_group, block_count, TAPS)
    offsets = jnp.arange(TAPS, dtype=jnp.float32)
    mode_weight = residues * jnp.sqrt(2.0 * decay_rates)
    impulse = jnp.einsum("gm,gmt->gt", mode_weight, jnp.exp(-decay_rates[:, :, None] * offsets))
    within_rows = toeplitz_rows(impulse)[:, :, TAPS:]
    within = jnp.einsum("gts,gkbs->gkbt", within_rows, blocks)
    to_end = jnp.exp(-decay_rates[:, :, None] * (TAPS - 1.0 - offsets))
    block_end = jnp.einsum("gms,gkbs->gkbm", to_end, blocks)
    block_decay = jnp.broadcast_to(jnp.exp(-decay_rates * TAPS)[:, None, None, :], block_end.shape)
    after_block, unused_decay = lax.associative_scan(chain_blocks, (block_end, block_decay), axis=2)
    entering = jnp.concatenate(
        [jnp.zeros_like(after_block[:, :, :1]), after_block[:, :, :-1]], axis=2
    )
    from_start = mode_weight[:, :, None] * jnp.exp(-decay_rates[:, :, None] * (offsets + 1.0))
    carried = jnp.einsum("gmt,gkbm->gkbt", from_start, entering)
    return ((within + carried).reshape(group_count, per_group, length), after_block[:, :, -1])


def per_device(
    hidden,
    norm_gain_a,
    in_weight_a,
    mr_filter,
    out_weight_a,
    norm_gain_b,
    in_weight_b,
    li_rate,
    li_residue,
    out_weight_b,
):
    gathered = collect(hidden, "tp", 1)
    first_gate, medium_in = layer_inputs(gathered, norm_gain_a, in_weight_a)
    medium = medium_conv(medium_in, mr_filter)
    gated_medium = (first_gate * medium).astype(jnp.bfloat16)
    first_partial = out_project(gated_medium, out_weight_a)
    first_summed = sent_and_summed(first_partial.astype(jnp.bfloat16), "tp", 1)
    after_a = (hidden.astype(jnp.float32) + first_summed).astype(jnp.bfloat16)
    gathered_next = collect(after_a, "tp", 1)
    second_gate, long_in = layer_inputs(gathered_next, norm_gain_b, in_weight_b)
    by_channel = lax.all_to_all(long_in, CTX, split_axis=0, concat_axis=1, tiled=True)
    channel_count, full_length = by_channel.shape
    groups_here = max(1, channel_count // GROUP)
    per_group = channel_count // groups_here
    first_group = lax.axis_index(CTX) * channel_count // GROUP
    rates_here = lax.dynamic_slice_in_dim(li_rate, first_group, groups_here, 0)
    residues_here = lax.dynamic_slice_in_dim(li_residue, first_group, groups_here, 0)
    long_whole, unused_end = long_parts(
        by_channel.reshape(groups_here, per_group, full_length), rates_here, residues_here
    )
    long_out = lax.all_to_all(
        long_whole.reshape(channel_count, full_length).astype(jnp.bfloat16),
        CTX,
        split_axis=1,
        concat_axis=0,
        tiled=True,
    ).astype(jnp.float32)
    gated_long = (second_gate * long_out).astype(jnp.bfloat16)
    second_partial = out_project(gated_long, out_weight_b)
    second_summed = sent_and_summed(second_partial.astype(jnp.bfloat16), "tp", 1)
    mixed = (after_a.astype(jnp.float32) + second_summed).astype(jnp.bfloat16)
    return (mixed, gated_medium, gated_long)


def solution(mesh):
    split = Mesh(mesh.devices.reshape(2, 4, 8, mesh.shape["tp"]), ("ctx_0", "ctx_1", "ctx_2", "tp"))
    in_specs = (
        P(CTX, "tp"),
        P(),
        P(None, CTX, "tp"),
        P("tp", None),
        P("tp", CTX),
        P(),
        P(None, CTX, "tp"),
        P("tp", None),
        P("tp", None),
        P("tp", CTX),
    )
    out_specs = (P(CTX, "tp"), P("tp", CTX), P("tp", CTX))
    return jax.shard_map(
        per_device, mesh=split, in_specs=in_specs, out_specs=out_specs, check_vma=False
    )
```

profile of v0, /device:TPU:1, one launch (start us, length us, event | category | flops | bytes accessed | tf_op | source)
XLA Modules:
  0.0 450.9 jit_solution(16483814376759491080)
XLA Ops:
  7.2 6.6 %all-gather = bf16[6,32,512]{2,1,0:T(8,128)(2,1)S(1)} all-gather(bf16[3,32,512]{2,1,0:T(8,128)(2,1)} %param.12), channel_id=2, replica_groups=mesh['ctx_0'=2,'ctx_1'=4,'ctx_2'=8,'tp'=4] {'ctx_0'}, dimensions={0}, use_global_device_ids=true | all-gather | bytes 294912 | tf_op jit(solution)/shard_map/all_gather | solution.py:21
  13.9 13.3 %all_gather.25 = bf16[8,3,32,512]{3,2,1,0:T(8,128)(2,1)} all-gather(bf16[2,3,32,512]{3,2,1,0:T(8,128)(2,1)S(1)} %bitcast.150), channel_id=1, replica_groups=mesh['ctx_0'=2,'ctx_1'=4,'ctx_2'=8,'tp'=4] {'ctx_1'}, dimensions={0}, use_global_device_ids=true | all-gather | bytes 983040 | tf_op jit(solution)/shard_map/all_gather | solution.py:21
  27.3 0.7 all-gather.9.cloned.1.call-update
  28.0 5.6 %all-gather.1 = bf16[6,32,512]{2,1,0:T(8,128)(2,1)S(1)} all-gather(bf16[3,32,512]{2,1,0:T(8,128)(2,1)S(1)} %copy-done.2), channel_id=3, replica_groups=mesh['ctx_0'=2,'ctx_1'=4,'ctx_2'=8,'tp'=4] {'ctx_0'}, dimensions={0}, use_global_device_ids=true | all-gather | bytes 294912 | tf_op jit(solution)/shard_map/all_gather | solution.py:21
  33.7 11.3 %all_gather.29 = bf16[8,3,32,512]{3,2,1,0:T(8,128)(2,1)} all-gather(bf16[2,3,32,512]{3,2,1,0:T(8,128)(2,1)S(1)} %bitcast.151), channel_id=1, replica_groups=mesh['ctx_0'=2,'ctx_1'=4,'ctx_2'=8,'tp'=4] {'ctx_1'}, dimensions={0}, use_global_device_ids=true | all-gather | bytes 983040 | tf_op jit(solution)/shard_map/all_gather | solution.py:21
  45.0 1.1 broadcast_in_dim.16
  46.1 12.8 %all-to-all-start = ((bf16[4,256,512]{2,1,0:T(8,128)(2,1)}), bf16[4,256,512]{2,1,0:T(8,128)(2,1)S(1)}, u32[]{:S(2)}, u32[]{:S(2)}) async-start(bf16[4,256,512]{2,1,0:T(8,128)(2,1)} %broadcast_in_dim.16), calls=%async_computation | async-start | bytes 2097152 | tf_op jit(solution)/shard_map/all_to_all | solution.py:40
  59.0 13.4 %all-to-all-done = bf16[4,256,512]{2,1,0:T(8,128)(2,1)S(1)} async-done(((bf16[4,256,512]{2,1,0:T(8,128)(2,1)}), bf16[4,256,512]{2,1,0:T(8,128)(2,1)S(1)}, u32[]{:S(2)}, u32[]{:S(2)}) %all-to-all-start) | async-done | bytes 1048608 | tf_op jit(solution)/shard_map/all_to_all | solution.py:40
  73.6 33.6 %all-gather.7.cloned.1.call-done = bf16[64,3,32,512]{3,2,1,0:T(8,128)(2,1)} async-done(((bf16[8,3,32,512]{3,2,1,0:T(8,128)(2,1)}), bf16[64,3,32,512]{3,2,1,0:T(8,128)(2,1)}) %all-gather.7.cloned.1.call-update) | async-done | bytes 6291472 | tf_op jit(solution)/shard_map/all_gather | solution.py:21
  107.2 3.6 copy.84
  110.8 1.8 convolution_bitcast_fusion.1
  112.7 1.4 collective-permute-start
  114.1 2.0 tile.20
  116.1 6.2 %tile.21 = bf16[32,32896]{1,0:T(8,128)(2,1)} reshape(bf16[32,128,257]{2,1,0:T(8,128)(2,1)} %tile.20) | data formatting | bytes 4210688 | tf_op jit(solution)/shard_map/tile | solution.py:94
  122.3 1.6 slice-done
  123.9 1.8 copy.111
  126.6 1.1 copy-done
  127.7 0.8 fusion.6
  129.1 95.2 %all-gather.9.cloned.1.call-done = bf16[512,2048]{0,1:T(8,128)(2,1)} async-done(((bf16[512,32]{0,1:T(8,128)(2,1)}), bf16[512,2048]{0,1:T(8,128)(2,1)}) %all-gather.9.cloned.1.call-update) | async-done | bytes 2097168 | tf_op jit(solution)/shard_map/all_gather | solution.py:79
  224.4 2.3 convolution_convert_fusion.1
  226.8 20.6 %all_to_all.43 = bf16[4,256,512]{2,1,0:T(8,128)(2,1)S(1)} all-to-all(bf16[4,256,512]{2,1,0:T(8,128)(2,1)S(1)} %bitcast.140), channel_id=1, replica_groups=mesh['ctx_0'=2,'ctx_1'=4,'ctx_2'=8,'tp'=4] {'tp'}, dimensions={0} | all-to-all | bytes 2097152 | tf_op jit(solution)/shard_map/all_to_all | solution.py:54
  247.7 1.1 broadcast_in_dim.20
  248.7 4.1 all-to-all-start.2
  253.7 47.3 %all-gather.11.cloned.1.call-done = bf16[64,3,32,512]{3,2,1,0:T(8,128)(2,1)} async-done(((bf16[8,3,32,512]{3,2,1,0:T(8,128)(2,1)}), bf16[64,3,32,512]{3,2,1,0:T(8,128)(2,1)}) %all-gather.11.cloned.1.call-update) | async-done | bytes 6291472 | tf_op jit(solution)/shard_map/all_gather | solution.py:21
  301.0 6.6 %copy.93 = bf16[2,4,8,3,32,512]{5,4,2,1,0,3:T(8,128)(2,1)} copy(bf16[2,4,8,3,32,512]{5,4,3,0,1,2:T(8,128)(2,1)} %bitcast.135) | data formatting | bytes 12582912 | tf_op jit(solution)/shard_map/transpose | solution.py:25
  308.8 4.6 %convolution_bitcast_fusion = f32[3,512,256]{1,2,0:T(8,128)S(1)} fusion(bf16[256,2048,1]{0,1,2:T(8,128)(2,1)S(1)} %bitcast.138, bf16[3,2048,512]{2,1,0:T(8,128)(2,1)} %bitcast.131), kind=kOutput, calls=%fused_computation.16 | convolution fusion | flops 1610612736 | bytes 8912896 | tf_op jit(solution)/shard_map/knc,tn->kct/dot_general | solution.py:66
  313.4 0.8 copy.95
  314.3 9.9 %all-to-all-start.3 = ((bf16[64,8,256]{2,1,0:T(8,128)(2,1)}), bf16[64,8,256]{2,1,0:T(8,128)(2,1)S(1)}, u32[]{:S(2)}, u32[]{:S(2)}) async-start(bf16[64,8,256]{2,1,0:T(8,128)(2,1)} %bitcast.25), calls=%async_computation.3 | async-start | bytes 524288 | tf_op jit(solution)/shard_map/all_to_all | solution.py:157
  325.6 11.8 %all-to-all-done.3 = bf16[64,8,256]{2,1,0:T(8,128)(2,1)S(1)} async-done(((bf16[64,8,256]{2,1,0:T(8,128)(2,1)}), bf16[64,8,256]{2,1,0:T(8,128)(2,1)S(1)}, u32[]{:S(2)}, u32[]{:S(2)}) %all-to-all-start.3) | async-done | bytes 262176 | tf_op jit(solution)/shard_map/all_to_all | solution.py:157
  337.7 1.2 slice.197
  338.9 1.2 slice.199
  344.5 1.1 slice.240
  349.5 0.7 pad.51
  350.2 0.8 pad.53
  351.2 0.8 pad.52
  352.2 1.1 pad.54
  353.2 1.1 pad.55
  354.3 1.6 pad.112
  356.1 1.6 pad.81
  358.6 18.9 %all_to_all.44 = bf16[8,64,256]{2,0,1:T(8,128)(2,1)S(1)} all-to-all(bf16[8,64,256]{2,0,1:T(8,128)(2,1)S(1)} %copy.97), channel_id=1, replica_groups=mesh['ctx_0'=2,'ctx_1'=4,'ctx_2'=8,'tp'=4] {'ctx_0','ctx_1','ctx_2'}, dimensions={1} | all-to-all | bytes 524288 | tf_op jit(solution)/shard_map/all_to_all | solution.py:167
  377.9 40.8 %all-gather.13.cloned.1.call-done = bf16[512,2048]{0,1:T(8,128)(2,1)} async-done(((bf16[512,32]{0,1:T(8,128)(2,1)}), bf16[512,2048]{0,1:T(8,128)(2,1)}) %all-gather.13.cloned.1.call-update) | async-done | bytes 2097168 | tf_op jit(solution)/shard_map/all_gather | solution.py:79
  418.7 2.3 convolution_convert_fusion
  421.0 1.1 copy.116
  422.1 7.9 %all-to-all-start.5 = ((bf16[4,256,512]{2,1,0:T(8,128)(2,1)}), bf16[4,256,512]{2,1,0:T(8,128)(2,1)S(1)}, u32[]{:S(2)}, u32[]{:S(2)}) async-start(bf16[4,256,512]{2,1,0:T(8,128)(2,1)} %bitcast.122), calls=%async_computation.5 | async-start | bytes 2097152 | tf_op jit(solution)/shard_map/all_to_all | solution.py:54
  430.0 0.8 copy.100
  430.8 0.8 copy.101
  431.6 11.8 %all-to-all-done.5 = bf16[4,256,512]{2,1,0:T(8,128)(2,1)S(1)} async-done(((bf16[4,256,512]{2,1,0:T(8,128)(2,1)}), bf16[4,256,512]{2,1,0:T(8,128)(2,1)S(1)}, u32[]{:S(2)}, u32[]{:S(2)}) %all-to-all-start.5) | async-done | bytes 1048608 | tf_op jit(solution)/shard_map/all_to_all | solution.py:54
  443.6 0.8 add_convert_fusion
  (126 shorter events, 17.1 us)
Async XLA Ops:
  7.2 20.8 %copy-start.2 = (bf16[3,32,512]{2,1,0:T(8,128)(2,1)S(1)}, bf16[3,32,512]{2,1,0:T(8,128)(2,1)}, u32[]{:S(2)}) copy-start(bf16[3,32,512]{2,1,0:T(8,128)(2,1)} %param.16) | copy-start | bytes 294916
  7.2 37.8 %copy-start.1 = (bf16[256,512]{1,0:T(8,128)(2,1)S(1)}, bf16[256,512]{1,0:T(8,128)(2,1)}, u32[]{:S(2)}) copy-start(bf16[256,512]{1,0:T(8,128)(2,1)} %param.10) | copy-start | bytes 786436
  7.2 100.0 %all-gather.7.cloned.1.call-start = ((), (), s32[]{:S(2)}) async-start(), calls=%async_computation.6 | async-start | bytes 7077888 | tf_op jit(solution)/shard_map/all_gather | solution.py:21
  27.2 197.1 %all-gather.9.cloned.1.call-start = ((), (), s32[]{:S(2)}) async-start(), calls=%async_computation.7 | async-start | bytes 2129920 | tf_op jit(solution)/shard_map/all_gather | solution.py:79
  28.0 273.0 %all-gather.11.cloned.1.call-start = ((), (), s32[]{:S(2)}) async-start(), calls=%async_computation.8 | async-start | bytes 7077888 | tf_op jit(solution)/shard_map/all_gather | solution.py:21
  45.0 13.9 %copy-start.3 = (f32[2048]{0:T(1024)S(1)}, f32[2048]{0:T(1024)}, u32[]{:S(2)}) copy-start(f32[2048]{0:T(1024)} %param.11) | copy-start | bytes 24580
  45.0 13.9 %copy-start.4 = (bf16[32,128]{1,0:T(8,128)(2,1)S(1)}, bf16[32,128]{1,0:T(8,128)(2,1)}, u32[]{:S(2)}) copy-start(bf16[32,128]{1,0:T(8,128)(2,1)} %param.13) | copy-start | bytes 24580
  46.1 26.3 %all-to-all-start = ((bf16[4,256,512]{2,1,0:T(8,128)(2,1)}), bf16[4,256,512]{2,1,0:T(8,128)(2,1)S(1)}, u32[]{:S(2)}, u32[]{:S(2)}) async-start(bf16[4,256,512]{2,1,0:T(8,128)(2,1)} %broadcast_in_dim.16), calls=%async_computation | async-start | bytes 2097152 | tf_op jit(solution)/shard_map/all_to_all | solution.py:40
  112.7 13.1 %collective-permute-start = (bf16[512,128]{0,1:T(8,128)(2,1)S(1)}, bf16[512,128]{0,1:T(8,128)(2,1)S(1)}, u32[]{:S(2)}, u32[]{:S(2)}) collective-permute-start(bf16[512,128]{0,1:T(8,128)(2,1)S(1)} %slice.245), channel_id=1, source_target_pairs={{0,4},{4,8},{8,12},{12,16},{16,20},{20,24},{24,28},{28,32},{32,36}... | collective-permute-start | bytes 393224 | tf_op jit(solution)/shard_map/ppermute | solution.py:35
  122.3 1.6 slice-start
  126.1 1.6 copy-start
  247.6 5.9 %copy-start.5 = (f32[2048]{0:T(1024)S(1)}, f32[2048]{0:T(1024)}, u32[]{:S(2)}) copy-start(f32[2048]{0:T(1024)} %param.15) | copy-start | bytes 24580
  247.6 5.9 %copy-start.6 = (f32[32,16]{0,1:T(8,128)S(1)}, f32[32,16]{0,1:T(8,128)}, u32[]{:S(2)}) copy-start(f32[32,16]{0,1:T(8,128)} %param.17) | copy-start | bytes 6148
  247.6 5.9 %copy-start.7 = (f32[32,16]{0,1:T(8,128)S(1)}, f32[32,16]{0,1:T(8,128)}, u32[]{:S(2)}) copy-start(f32[32,16]{0,1:T(8,128)} %param.18) | copy-start | bytes 6148
  248.7 58.8 %all-to-all-start.2 = ((bf16[4,256,512]{2,1,0:T(8,128)(2,1)}), bf16[4,256,512]{2,1,0:T(8,128)(2,1)S(1)}, u32[]{:S(2)}, u32[]{:S(2)}) async-start(bf16[4,256,512]{2,1,0:T(8,128)(2,1)} %broadcast_in_dim.20), calls=%async_computation.2 | async-start | bytes 2097152 | tf_op jit(solution)/shard_map/all_to_all | solution.py:40
  252.9 165.8 %all-gather.13.cloned.1.call-start = ((), (), s32[]{:S(2)}) async-start(), calls=%async_computation.9 | async-start | bytes 2129920 | tf_op jit(solution)/shard_map/all_gather | solution.py:79
  314.3 23.1 %all-to-all-start.3 = ((bf16[64,8,256]{2,1,0:T(8,128)(2,1)}), bf16[64,8,256]{2,1,0:T(8,128)(2,1)S(1)}, u32[]{:S(2)}, u32[]{:S(2)}) async-start(bf16[64,8,256]{2,1,0:T(8,128)(2,1)} %bitcast.25), calls=%async_computation.3 | async-start | bytes 524288 | tf_op jit(solution)/shard_map/all_to_all | solution.py:157
  422.1 21.4 %all-to-all-start.5 = ((bf16[4,256,512]{2,1,0:T(8,128)(2,1)}), bf16[4,256,512]{2,1,0:T(8,128)(2,1)S(1)}, u32[]{:S(2)}, u32[]{:S(2)}) async-start(bf16[4,256,512]{2,1,0:T(8,128)(2,1)} %bitcast.122), calls=%async_computation.5 | async-start | bytes 2097152 | tf_op jit(solution)/shard_map/all_to_all | solution.py:54
Sparse Core Ops, SparseCore 0:
  27.3 79.8 all-gather.6
  110.7 113.6 all-gather.8
  226.1 74.8 all-gather.10
  304.4 114.2 all-gather.12
where the time goes:
time: 452 us; the launch traced here: 451 us
  waiting for transfers between devices  255 us (56%)
  blocking collectives  76.5 us (17%)
  local copies, waits for them, and re-layouts  50.8 us (11%)
  starting transfers between devices  36.2 us (8%)
  between operations  14.5 us (3%)
  matrix products  12.8 us (3%)
  other arithmetic  4.99 us (1%)
    all_gather x2, waiting for transfers between devices, out_project(): lax.all_gather(weight, CTX, axis=1, tiled=True)  136 us
    all_gather x2, waiting for transfers between devices, gather_in_order(): blocks = lax.all_gather(blocks, axes[k], axis=0, tiled=True)  80.9 us
    all_gather x4, blocking collectives, gather_in_order(): blocks = lax.all_gather(blocks, axes[k], axis=0, tiled=True)  36.9 us
    all_to_all x1, blocking collectives, sent_and_summed(): lax.all_to_all(cut_along(shard, dim, peers), axis, 0, 0, tiled=True)  20.6 us
    all_to_all x1, blocking collectives, per_device(): lax.all_to_all(long_whole.reshape(channel_count, full_length).astype(jnp....  18.9 us
    all_to_all x2, starting transfers between devices, from_everyone(): return lax.all_to_all(copies, axis, split_axis=0, concat_axis=0, tiled=True)  16.9 us
    all_to_all x2, waiting for transfers between devices, from_everyone(): return lax.all_to_all(copies, axis, split_axis=0, concat_axis=0, tiled=True)  13.4 us
    all_to_all x1, waiting for transfers between devices, per_device(): lax.all_to_all(long_in, CTX, split_axis=0, concat_axis=1, tiled=True)  11.8 us
  transfers between devices with their start and end apart: 9, of which 7 were waited for; matrix products, arithmetic and copies ran while one was open for 14% of the time, Pallas kernels for 0%

commit v1 on v0

--- a/solution.py
+++ b/solution.py
@@ -76,7 +76,9 @@
     return jnp.einsum(
         "ct,cn->tn",
         gated,
-        lax.all_gather(weight, CTX, axis=1, tiled=True),
+        jnp.concatenate(
+            lax.all_to_all(jnp.stack([weight] * lax.axis_size(CTX)), CTX, 0, 0), axis=1
+        ),
         preferred_element_type=jnp.float32,
     )
 

time: 452 us -> 500 us (1.11); the launches traced: 451 us -> 493 us
  waiting for transfers between devices: 255 us -> 148 us
  local copies, waits for them, and re-layouts: 50.8 us -> 133 us
  other arithmetic: 4.99 us -> 39.8 us
  blocking collectives: 76.5 us -> 98.2 us
  starting transfers between devices: 36.2 us -> 44.6 us
    all_gather x2 -> x0, waiting for transfers between devices: 136 us -> none  [out_project(): lax.all_gather(weight, CTX, axis=1, tiled=True)]
    all_to_all x0 -> x2, waiting for transfers between devices: none -> 44 us  [out_project(): lax.all_to_all(jnp.stack([weight] * lax.axis_size(CTX)), CTX, 0, 0)]
    pad x10, local copies, waits for them, and re-layouts: 7.4 us -> 48.1 us  [long_parts(): lax.associative_scan(chain_blocks, (block_end, block_decay), axis=2)]
    all_to_all x0 -> x1, blocking collectives: none -> 25.5 us  [from_everyone(): return lax.all_to_all(copies, axis, split_axis=0, concat_axis=0, tiled=True)]
    slice x17, local copies, waits for them, and re-layouts: 7.44 us -> 27.2 us  [long_parts(): lax.associative_scan(chain_blocks, (block_end, block_decay), axis=2)]
    all_to_all x0 -> x2, starting transfers between devices: none -> 19.2 us  [out_project(): lax.all_to_all(jnp.stack([weight] * lax.axis_size(CTX)), CTX, 0, 0)]
    all_to_all x2 -> x1, waiting for transfers between devices: 13.4 us -> 0.01 us  [from_everyone(): return lax.all_to_all(copies, axis, split_axis=0, concat_axis=0, tiled=True)]
    add x12, other arithmetic: 0.94 us -> 13.7 us  [chain_blocks(): return (earlier[0] * latter[1] + latter[0], earlier[1] * latter[1])]
  transfers between devices with their start and end apart: 9 -> 8, of which waited for: 7 -> 5; matrix products, arithmetic and copies ran while one was open for 14% -> 10% of each run, Pallas kernels for 0% -> 0%
where the time goes in v1:
time: 500 us; the launch traced here: 493 us
  waiting for transfers between devices  148 us (30%)
  local copies, waits for them, and re-layouts  133 us (27%)
  blocking collectives  98.2 us (20%)
  starting transfers between devices  44.6 us (9%)
  other arithmetic  39.8 us (8%)
  matrix products  15.1 us (3%)
  between operations  14.6 us (3%)
    all_gather x2, waiting for transfers between devices, gather_in_order(): blocks = lax.all_gather(blocks, axes[k], axis=0, tiled=True)  91.9 us
    pad x10, local copies, waits for them, and re-layouts, long_parts(): lax.associative_scan(chain_blocks, (block_end, block_decay), axis=2)  48.1 us
    all_to_all x2, waiting for transfers between devices, out_project(): lax.all_to_all(jnp.stack([weight] * lax.axis_size(CTX)), CTX, 0, 0)  44 us
    all_gather x4, blocking collectives, gather_in_order(): blocks = lax.all_gather(blocks, axes[k], axis=0, tiled=True)  36.9 us
    slice x17, local copies, waits for them, and re-layouts, long_parts(): lax.associative_scan(chain_blocks, (block_end, block_decay), axis=2)  27.2 us
    all_to_all x1, blocking collectives, from_everyone(): return lax.all_to_all(copies, axis, split_axis=0, concat_axis=0, tiled=True)  25.5 us
    all_to_all x2, starting transfers between devices, out_project(): lax.all_to_all(jnp.stack([weight] * lax.axis_size(CTX)), CTX, 0, 0)  19.2 us
    all_to_all x1, blocking collectives, per_device(): lax.all_to_all(long_whole.reshape(channel_count, full_length).astype(jnp....  18.3 us
  transfers between devices with their start and end apart: 8, of which 5 were waited for; matrix products, arithmetic and copies ran while one was open for 10% of the time, Pallas kernels for 0%

profile of v1, /device:TPU:1, one launch (start us, length us, event | category | flops | bytes accessed | tf_op | source)
XLA Modules:
  0.0 493.3 jit_solution(9241194101817750048)
XLA Ops:
  7.2 6.6 %all-gather = bf16[6,32,512]{2,1,0:T(8,128)(2,1)S(1)} all-gather(bf16[3,32,512]{2,1,0:T(8,128)(2,1)} %param.12), channel_id=2, replica_groups=mesh['ctx_0'=2,'ctx_1'=4,'ctx_2'=8,'tp'=4] {'ctx_0'}, dimensions={0}, use_global_device_ids=true | all-gather | bytes 294912 | tf_op jit(solution)/shard_map/all_gather | solution.py:21
  13.9 13.3 %all_gather.19 = bf16[8,3,32,512]{3,2,1,0:T(8,128)(2,1)} all-gather(bf16[2,3,32,512]{3,2,1,0:T(8,128)(2,1)S(1)} %bitcast.161), channel_id=1, replica_groups=mesh['ctx_0'=2,'ctx_1'=4,'ctx_2'=8,'tp'=4] {'ctx_1'}, dimensions={0}, use_global_device_ids=true | all-gather | bytes 983040 | tf_op jit(solution)/shard_map/all_gather | solution.py:21
  27.3 5.6 %all-gather.1 = bf16[6,32,512]{2,1,0:T(8,128)(2,1)S(1)} all-gather(bf16[3,32,512]{2,1,0:T(8,128)(2,1)S(1)} %copy-done.5), channel_id=3, replica_groups=mesh['ctx_0'=2,'ctx_1'=4,'ctx_2'=8,'tp'=4] {'ctx_0'}, dimensions={0}, use_global_device_ids=true | all-gather | bytes 294912 | tf_op jit(solution)/shard_map/all_gather | solution.py:21
  32.9 11.3 %all_gather.22 = bf16[8,3,32,512]{3,2,1,0:T(8,128)(2,1)} all-gather(bf16[2,3,32,512]{3,2,1,0:T(8,128)(2,1)S(1)} %bitcast.162), channel_id=1, replica_groups=mesh['ctx_0'=2,'ctx_1'=4,'ctx_2'=8,'tp'=4] {'ctx_1'}, dimensions={0}, use_global_device_ids=true | all-gather | bytes 983040 | tf_op jit(solution)/shard_map/all_gather | solution.py:21
  44.4 25.5 %all_to_all.53 = bf16[4,256,512]{2,1,0:T(8,128)(2,1)S(1)} all-to-all(bf16[4,256,512]{2,1,0:T(8,128)(2,1)S(1)} %broadcast_in_dim.16), channel_id=1, replica_groups=mesh['ctx_0'=2,'ctx_1'=4,'ctx_2'=8,'tp'=4] {'tp'}, dimensions={0} | all-to-all | bytes 2097152 | tf_op jit(solution)/shard_map/all_to_all | solution.py:40
  71.4 12.7 %all-to-all-start.1 = ((bf16[64,512,32]{1,2,0:T(8,128)(2,1)}), bf16[64,512,32]{1,2,0:T(8,128)(2,1)}, u32[]{:S(2)}, u32[]{:S(2)}) async-start(bf16[64,512,32]{1,2,0:T(8,128)(2,1)} %stack.4), calls=%async_computation.1 | async-start | bytes 4194304 | tf_op jit(solution)/shard_map/all_to_all | solution.py:80
  85.6 66.2 %all-gather.5.cloned.1.call-done = bf16[64,3,32,512]{3,2,1,0:T(8,128)(2,1)} async-done(((bf16[8,3,32,512]{3,2,1,0:T(8,128)(2,1)}), bf16[64,3,32,512]{3,2,1,0:T(8,128)(2,1)}) %all-gather.5.cloned.1.call-update) | async-done | bytes 6291472 | tf_op jit(solution)/shard_map/all_gather | solution.py:21
  151.7 3.6 copy.96
  155.3 1.8 convolution_bitcast_fusion.1
  158.6 2.0 tile.20
  160.6 6.2 %tile.21 = bf16[32,32896]{1,0:T(8,128)(2,1)} reshape(bf16[32,128,257]{2,1,0:T(8,128)(2,1)} %tile.20) | data formatting | bytes 4210688 | tf_op jit(solution)/shard_map/tile | solution.py:96
  168.4 1.8 copy.126
  174.0 2.4 convolution_convert_fusion.1
  176.5 17.5 %all_to_all.54 = bf16[4,256,512]{2,1,0:T(8,128)(2,1)S(1)} all-to-all(bf16[4,256,512]{2,1,0:T(8,128)(2,1)S(1)} %bitcast.150), channel_id=1, replica_groups=mesh['ctx_0'=2,'ctx_1'=4,'ctx_2'=8,'tp'=4] {'tp'}, dimensions={0} | all-to-all | bytes 2097152 | tf_op jit(solution)/shard_map/all_to_all | solution.py:54
  196.0 4.9 all-to-all-start.3
  201.1 25.7 %all-gather.7.cloned.1.call-done = bf16[64,3,32,512]{3,2,1,0:T(8,128)(2,1)} async-done(((bf16[8,3,32,512]{3,2,1,0:T(8,128)(2,1)}), bf16[64,3,32,512]{3,2,1,0:T(8,128)(2,1)}) %all-gather.7.cloned.1.call-update) | async-done | bytes 6291472 | tf_op jit(solution)/shard_map/all_gather | solution.py:21
  226.8 6.5 %copy.105 = bf16[2,4,8,3,32,512]{5,4,2,1,0,3:T(8,128)(2,1)} copy(bf16[2,4,8,3,32,512]{5,4,3,0,1,2:T(8,128)(2,1)} %bitcast.144) | data formatting | bytes 12582912 | tf_op jit(solution)/shard_map/transpose | solution.py:25
  235.5 4.6 convolution_bitcast_fusion
  241.0 9.9 %all-to-all-start.4 = ((bf16[64,8,256]{2,1,0:T(8,128)(2,1)}), bf16[64,8,256]{2,1,0:T(8,128)(2,1)S(1)}, u32[]{:S(2)}, u32[]{:S(2)}) async-start(bf16[64,8,256]{2,1,0:T(8,128)(2,1)} %bitcast.160), calls=%async_computation.4 | async-start | bytes 524288 | tf_op jit(solution)/shard_map/all_to_all | solution.py:159
  257.6 6.3 %all-to-all-done.4 = bf16[64,8,256]{2,1,0:T(8,128)(2,1)S(1)} async-done(((bf16[64,8,256]{2,1,0:T(8,128)(2,1)}), bf16[64,8,256]{2,1,0:T(8,128)(2,1)S(1)}, u32[]{:S(2)}, u32[]{:S(2)}) %all-to-all-start.4) | async-done | bytes 262176 | tf_op jit(solution)/shard_map/all_to_all | solution.py:159
  266.5 1.8 slice.197
  268.3 1.8 slice.199
  275.1 1.8 slice.205
  276.9 1.8 slice.207
  281.9 1.7 slice.211
  294.6 1.7 fusion.53
  300.2 1.8 slice.234
  303.2 1.8 slice.240
  306.6 4.9 pad.46
  311.5 4.9 pad.47
  317.9 4.9 pad.49
  325.3 4.9 pad.48
  334.3 4.9 %pad.50 = f32[1,8,16,16]{2,3,1,0:T(8,128)} pad(f32[1,8,8,16]{2,3,1,0:T(8,128)} %pad_maximum_fusion.3, f32[]{:T(128)} %constant.21.clone.1), padding=0_0_0x0_0_0x0_1_1x0_0_0 | pad | bytes 12292 | tf_op jit(solution)/shard_map/pad | solution.py:129
  339.2 4.9 %pad.51 = f32[1,8,16,16]{2,3,1,0:T(8,128)} pad(f32[1,8,8,16]{2,3,1,0:T(8,128)} %add.154, f32[]{:T(128)} %constant.21.clone.1), padding=0_0_0x0_0_0x1_0_1x0_0_0 | pad | bytes 12292 | tf_op jit(solution)/shard_map/pad | solution.py:129
  345.7 5.0 %pad.53 = f32[1,8,32,16]{2,3,1,0:T(8,128)} pad(f32[1,8,16,16]{2,3,1,0:T(8,128)} %add.156, f32[]{:T(128)} %constant.21.clone.1), padding=0_0_0x0_0_0x1_0_1x0_0_0 | pad | bytes 24580 | tf_op jit(solution)/shard_map/pad | solution.py:129
  353.2 5.0 %pad.52 = f32[1,8,32,16]{2,3,1,0:T(8,128)} pad(f32[1,8,16,16]{2,3,1,0:T(8,128)} %pad_maximum_fusion.4, f32[]{:T(128)} %constant.21.clone.1), padding=0_0_0x0_0_0x0_1_1x0_0_0 | pad | bytes 24580 | tf_op jit(solution)/shard_map/pad | solution.py:129
  361.5 3.4 pad.54
  364.9 5.2 %pad.55 = f32[1,8,64,16]{2,3,1,0:T(8,128)} pad(f32[1,8,32,16]{2,3,1,0:T(8,128)} %add.158, f32[]{:T(128)} %constant.21.clone.1), padding=0_0_0x0_0_0x1_0_1x0_0_0 | pad | bytes 49156 | tf_op jit(solution)/shard_map/pad | solution.py:129
  371.5 5.4 %pad.112 = f32[1,8,128,16]{2,3,1,0:T(8,128)} pad(f32[1,8,64,16]{2,3,1,0:T(8,128)} %add.160, f32[]{:T(128)} %constant.21.clone.1), padding=0_0_0x0_0_0x1_0_1x0_0_0 | pad | bytes 98308
  384.4 18.3 %all_to_all.55 = bf16[8,64,256]{2,0,1:T(8,128)(2,1)S(1)} all-to-all(bf16[8,64,256]{2,0,1:T(8,128)(2,1)S(1)} %copy.109), channel_id=1, replica_groups=mesh['ctx_0'=2,'ctx_1'=4,'ctx_2'=8,'tp'=4] {'ctx_0','ctx_1','ctx_2'}, dimensions={1} | all-to-all | bytes 524288 | tf_op jit(solution)/shard_map/all_to_all | solution.py:169
  404.2 6.4 %all-to-all-start.6 = ((bf16[64,512,32]{1,2,0:T(8,128)(2,1)}), bf16[64,512,32]{1,2,0:T(8,128)(2,1)}, u32[]{:S(2)}, u32[]{:S(2)}) async-start(bf16[64,512,32]{1,2,0:T(8,128)(2,1)} %stack.5), calls=%async_computation.6 | async-start | bytes 4194304 | tf_op jit(solution)/shard_map/all_to_all | solution.py:80
  411.7 2.0 copy.110
  413.8 44.0 %all-to-all-done.6 = bf16[64,512,32]{1,2,0:T(8,128)(2,1)} async-done(((bf16[64,512,32]{1,2,0:T(8,128)(2,1)}), bf16[64,512,32]{1,2,0:T(8,128)(2,1)}, u32[]{:S(2)}, u32[]{:S(2)}) %all-to-all-start.6) | async-done | bytes 2097184 | tf_op jit(solution)/shard_map/all_to_all | solution.py:80
  457.8 2.5 convolution_convert_fusion
  461.4 9.3 %all-to-all-start.7 = ((bf16[4,256,512]{2,1,0:T(8,128)(2,1)}), bf16[4,256,512]{2,1,0:T(8,128)(2,1)}, u32[]{:S(2)}, u32[]{:S(2)}) async-start(bf16[4,256,512]{2,1,0:T(8,128)(2,1)} %bitcast.149), calls=%async_computation.7 | async-start | bytes 2097152 | tf_op jit(solution)/shard_map/all_to_all | solution.py:54
  470.7 1.9 copy.133
  472.6 2.1 copy.113
  478.8 5.4 %all-to-all-done.7 = bf16[4,256,512]{2,1,0:T(8,128)(2,1)} async-done(((bf16[4,256,512]{2,1,0:T(8,128)(2,1)}), bf16[4,256,512]{2,1,0:T(8,128)(2,1)}, u32[]{:S(2)}, u32[]{:S(2)}) %all-to-all-start.7) | async-done | bytes 1048608 | tf_op jit(solution)/shard_map/all_to_all | solution.py:54
  (148 shorter events, 84.7 us)
Async XLA Ops:
  7.2 20.1 %copy-start.5 = (bf16[3,32,512]{2,1,0:T(8,128)(2,1)S(1)}, bf16[3,32,512]{2,1,0:T(8,128)(2,1)}, u32[]{:S(2)}) copy-start(bf16[3,32,512]{2,1,0:T(8,128)(2,1)} %param.16) | copy-start | bytes 294916
  7.2 37.1 %copy-start.4 = (bf16[256,512]{1,0:T(8,128)(2,1)S(1)}, bf16[256,512]{1,0:T(8,128)(2,1)}, u32[]{:S(2)}) copy-start(bf16[256,512]{1,0:T(8,128)(2,1)} %param.10) | copy-start | bytes 786436
  7.2 144.5 %all-gather.5.cloned.1.call-start = ((), (), s32[]{:S(2)}) async-start(), calls=%async_computation.8 | async-start | bytes 7077888 | tf_op jit(solution)/shard_map/all_gather | solution.py:21
  27.2 199.6 %all-gather.7.cloned.1.call-start = ((), (), s32[]{:S(2)}) async-start(), calls=%async_computation.9 | async-start | bytes 7077888 | tf_op jit(solution)/shard_map/all_gather | solution.py:21
  44.2 25.6 %copy-start.6 = (bf16[512,32]{0,1:T(8,128)(2,1)S(1)}, bf16[512,32]{0,1:T(8,128)(2,1)}, u32[]{:S(2)}) copy-start(bf16[512,32]{0,1:T(8,128)(2,1)} %param.14) | copy-start | bytes 98308
  71.4 12.8 %copy-start.8 = (f32[2048]{0:T(1024)S(1)}, f32[2048]{0:T(1024)}, u32[]{:S(2)}) copy-start(f32[2048]{0:T(1024)} %param.11) | copy-start | bytes 24580
  71.4 12.8 %copy-start.9 = (bf16[32,128]{1,0:T(8,128)(2,1)S(1)}, bf16[32,128]{1,0:T(8,128)(2,1)}, u32[]{:S(2)}) copy-start(bf16[32,128]{1,0:T(8,128)(2,1)} %param.13) | copy-start | bytes 24580
  71.4 102.5 %all-to-all-start.1 = ((bf16[64,512,32]{1,2,0:T(8,128)(2,1)}), bf16[64,512,32]{1,2,0:T(8,128)(2,1)}, u32[]{:S(2)}, u32[]{:S(2)}) async-start(bf16[64,512,32]{1,2,0:T(8,128)(2,1)} %stack.4), calls=%async_computation.1 | async-start | bytes 4194304 | tf_op jit(solution)/shard_map/all_to_all | solution.py:80
  157.2 13.0 %collective-permute-start = (bf16[512,128]{0,1:T(8,128)(2,1)S(1)}, bf16[512,128]{0,1:T(8,128)(2,1)S(1)}, u32[]{:S(2)}, u32[]{:S(2)}) collective-permute-start(bf16[512,128]{0,1:T(8,128)(2,1)S(1)} %slice.245), channel_id=1, source_target_pairs={{0,4},{4,8},{8,12},{12,16},{16,20},{20,24},{24,28},{28,32},{32,36}... | collective-permute-start | bytes 393224 | tf_op jit(solution)/shard_map/ppermute | solution.py:35
  166.8 1.6 slice-start
  170.6 1.6 copy-start
  173.3 3.0 copy-start.1
  194.1 6.7 %copy-start.10 = (f32[2048]{0:T(1024)S(1)}, f32[2048]{0:T(1024)}, u32[]{:S(2)}) copy-start(f32[2048]{0:T(1024)} %param.15) | copy-start | bytes 24580
  194.1 6.7 %copy-start.11 = (f32[32,16]{0,1:T(8,128)S(1)}, f32[32,16]{0,1:T(8,128)}, u32[]{:S(2)}) copy-start(f32[32,16]{0,1:T(8,128)} %param.17) | copy-start | bytes 6148
  194.1 6.7 %copy-start.12 = (f32[32,16]{0,1:T(8,128)S(1)}, f32[32,16]{0,1:T(8,128)}, u32[]{:S(2)}) copy-start(f32[32,16]{0,1:T(8,128)} %param.18) | copy-start | bytes 6148
  194.2 0.7 copy-start.2
  196.0 37.4 %all-to-all-start.3 = ((bf16[4,256,512]{2,1,0:T(8,128)(2,1)}), bf16[4,256,512]{2,1,0:T(8,128)(2,1)}, u32[]{:S(2)}, u32[]{:S(2)}) async-start(bf16[4,256,512]{2,1,0:T(8,128)(2,1)} %broadcast_in_dim.20), calls=%async_computation.3 | async-start | bytes 2097152 | tf_op jit(solution)/shard_map/all_to_all | solution.py:40
  201.1 50.9 %copy-start.15 = (f32[16]{0:T(128)}, f32[16]{0:T(128)S(1)}, u32[]{:S(2)}) copy-start(f32[16]{0:T(128)S(1)} %get-tuple-element.19) | copy-start | bytes 196
  201.1 50.9 %copy-start.17 = (f32[16]{0:T(128)}, f32[16]{0:T(128)S(1)}, u32[]{:S(2)}) copy-start(f32[16]{0:T(128)S(1)} %get-tuple-element.20) | copy-start | bytes 196
  241.0 22.9 %all-to-all-start.4 = ((bf16[64,8,256]{2,1,0:T(8,128)(2,1)}), bf16[64,8,256]{2,1,0:T(8,128)(2,1)S(1)}, u32[]{:S(2)}, u32[]{:S(2)}) async-start(bf16[64,8,256]{2,1,0:T(8,128)(2,1)} %bitcast.160), calls=%async_computation.4 | async-start | bytes 524288 | tf_op jit(solution)/shard_map/all_to_all | solution.py:159
  251.5 0.8 copy-start.14
  255.6 28.0 %copy-start.13 = (f32[16]{0:T(128)S(1)}, f32[16]{0:T(128)}, u32[]{:S(2)}) copy-start(f32[16]{0:T(128)} %get-tuple-element.32) | copy-start | bytes 196
  332.7 48.7 %copy-start.16 = (f32[16]{0:T(128)S(1)}, f32[16]{0:T(128)}, u32[]{:S(2)}) copy-start(f32[16]{0:T(128)} %copy-done.15) | copy-start | bytes 196
  379.6 23.1 %copy-start.7 = (bf16[512,32]{0,1:T(8,128)(2,1)S(1)}, bf16[512,32]{0,1:T(8,128)(2,1)}, u32[]{:S(2)}) copy-start(bf16[512,32]{0,1:T(8,128)(2,1)} %param.19) | copy-start | bytes 98308
  404.2 53.6 %all-to-all-start.6 = ((bf16[64,512,32]{1,2,0:T(8,128)(2,1)}), bf16[64,512,32]{1,2,0:T(8,128)(2,1)}, u32[]{:S(2)}, u32[]{:S(2)}) async-start(bf16[64,512,32]{1,2,0:T(8,128)(2,1)} %stack.5), calls=%async_computation.6 | async-start | bytes 4194304 | tf_op jit(solution)/shard_map/all_to_all | solution.py:80
  461.4 22.9 %all-to-all-start.7 = ((bf16[4,256,512]{2,1,0:T(8,128)(2,1)}), bf16[4,256,512]{2,1,0:T(8,128)(2,1)}, u32[]{:S(2)}, u32[]{:S(2)}) async-start(bf16[4,256,512]{2,1,0:T(8,128)(2,1)} %bitcast.149), calls=%async_computation.7 | async-start | bytes 2097152 | tf_op jit(solution)/shard_map/all_to_all | solution.py:54
  476.6 9.1 %copy-start.3 = (bf16[256,512]{1,0:T(8,128)(2,1)S(1)}, bf16[256,512]{1,0:T(8,128)(2,1)}, u32[]{:S(2)}) copy-start(bf16[256,512]{1,0:T(8,128)(2,1)} %copy-done.2) | copy-start | bytes 786436
Sparse Core Ops, SparseCore 0:
  27.3 124.3 all-gather.4
  153.5 73.2 all-gather.6
